TPU v7x, 256 devices: a whole 4x4x8 slice. The times are simulated.
256 devices in a mesh: wide: 32 (over x, y, core), narrow: 8 (over z).
Axes of the slice: x: 4, y: 4, z: 8, core: 2. Of those that a mesh axis runs over, the one named last changes fastest.
Arguments:
- panels: float32 [256, 512, 512], P('wide', 'narrow'), may hold values from -0.6 to 0.6
- factors: float32 [64, 512, 512], P('wide', 'narrow'), may hold values from -2 to 2
- member: int32 [64, 4], replicated, may hold values from 0 to 255, as said below
- target: int32 [64, 10], replicated, may hold values from 0 to 31
- ancestors: float32 [32, 512, 512], P('wide', 'narrow'), may hold values from -6 to 6
Outputs:
- updated: float32 [32, 512, 512], P('wide', 'narrow')
Inputs may be any that keep to these rules, and one draw needn't show every extreme that they name: `member`: the blocks of supernode s are 4 distinct indices in [(s // 2) * 8, (s // 2 + 1) * 8); every block belongs to exactly one supernode.
All inputs are finite; a program needn't handle non-finite values.
Results may differ from a plain program's by a relative error of at most 0.0003.
Values sent between devices are 32-bit elements; how exact they have to be, the bound alone decides.
No kernel may reach another device: no remote copies, remote signals or barrier semaphores. Data moves between devices by JAX's collectives and lax.ppermute only.
A program may use at most 128 MiB of HBM per device.

v0:
```python
import jax
import jax.numpy as jnp
import numpy as np
from jax import lax
from jax.sharding import PartitionSpec as P


def pair_lists(count):
    left_pick = []
    right_pick = []
    for upper in range(count):
        for lower in range(upper + 1):
            left_pick.append(upper)
            right_pick.append(lower)
    return (np.array(left_pick, dtype=np.int32), np.array(right_pick, dtype=np.int32))


def shards(panels, factors, member, target, ancestors):
    highest = lax.Precision.HIGHEST
    sup_count = factors.shape[0]
    blk_count = panels.shape[0]
    tile_count = ancestors.shape[0] * lax.axis_size("wide")
    left_pick, right_pick = pair_lists(member.shape[1])
    owner_index = lax.axis_index("wide")
    own_members = (
        lax.dynamic_slice_in_dim(member, owner_index * sup_count, sup_count, 0)
        - owner_index * blk_count
    )
    own_targets = lax.dynamic_slice_in_dim(target, owner_index * sup_count, sup_count, 0)
    full_factors = lax.all_gather(factors, "narrow", axis=1, tiled=True)
    blocks = panels[own_members]
    scaled = jnp.einsum("skrw,swv->skrv", blocks, full_factors, precision=highest)
    left_rows = scaled[:, left_pick]
    right_rows = lax.all_gather(scaled, "narrow", axis=2, tiled=True)[:, right_pick]
    updates = jnp.einsum("sprv,spmv->sprm", left_rows, right_rows, precision=highest)
    tile_ids = jnp.arange(tile_count, dtype=jnp.int32)
    onehot = (own_targets[:, :, None] == tile_ids[None, None, :]).astype(jnp.float32)
    portion = jnp.einsum("spa,sprw->arw", onehot, updates, precision=highest)
    totals = lax.psum_scatter(portion, "wide", scatter_dimension=0, tiled=True)
    return ancestors - totals


def solution(mesh):
    return jax.shard_map(
        shards,
        mesh=mesh,
        in_specs=(
            P("wide", "narrow", None),
            P("wide", "narrow", None),
            P(),
            P(),
            P("wide", "narrow", None),
        ),
        out_specs=P("wide", "narrow", None),
        check_vma=False,
    )
```

profile of v0, /device:TPU:2, one launch (start us, length us, event | category | flops | bytes accessed | tf_op | source)
XLA Modules:
  0.0 293.5 jit_solution(6393277430765025806)
XLA Ops:
  6.5 0.0 copy-start
  6.5 0.0 all-gather.3.cloned.1.call-start
  6.5 0.7 all-gather.3.cloned.1.call-update
  7.3 0.0 all-gather.5.cloned.1.call-start
  7.3 0.8 compare_select_fusion
  8.1 0.1 copy.15
  8.2 0.1 reshape.3
  8.3 0.0 copy-done
  8.3 0.6 gather_fusion
  8.9 44.1 %all-gather.3.cloned.1.call-done = f32[2,512,512]{2,1,0:T(8,128)} async-done(((f32[2,64,512]{2,1,0:T(8,128)}), f32[2,512,512]{2,1,0:T(8,128)}) %all-gather.3.cloned.1.call-update) | async-done | bytes 2097168 | tf_op jit(solution)/shard_map/all_gather | solution.py:30
  53.0 0.0 copy-start.3
  53.0 0.0 copy-start.5
  53.0 0.0 copy-start.4
  53.0 4.5 %fusion.8 = f32[2,4,64,512]{3,2,1,0:T(8,128)} fusion(f32[2,4,64,512]{3,2,1,0:T(8,128)S(1)} %bitcast.21, f32[2,512,512]{2,1,0:T(8,128)} %all-gather.3.cloned.1.call-done), kind=kOutput, calls=%fused_computation.9 | convolution fusion | flops 1610612736 | bytes 4194304 | tf_op jit(solution)/shard_map/skrw,swv->skrv/dot_general | solution.py:32
  57.5 0.0 copy-start.1
  57.5 0.0 all-gather.5.cloned.1.call-update
  57.6 0.0 reduce-scatter.2.cloned.1.call-start
  57.6 0.0 copy-done.3
  57.6 0.1 constant_dynamic-slice_fusion
  57.7 0.1 copy.14
  57.8 0.0 copy-done.5
  57.8 0.0 copy-done.4
  57.8 0.9 copy-done.1
  58.8 2.2 gather_fusion.1
  60.9 89.4 %all-gather.5.cloned.1.call-done = f32[2,4,512,512]{3,2,1,0:T(8,128)} async-done(((f32[2,4,64,512]{3,2,1,0:T(8,128)}), f32[2,4,512,512]{3,2,1,0:T(8,128)}) %all-gather.5.cloned.1.call-update) | async-done | bytes 8388624 | tf_op jit(solution)/shard_map/all_gather | solution.py:34
  150.3 12.6 %gather_fusion.2 = f32[10,2,512,512]{3,2,1,0:T(8,128)} fusion(f32[2,4,512,512]{3,2,1,0:T(8,128)} %all-gather.5.cloned.1.call-done, s32[1024]{0:T(1024)S(1)} %pad_clamp_fusion), kind=kCustom, calls=%fused_computation.2 | custom fusion | bytes 41943080 | tf_op jit(solution)/shard_map/gather | solution.py:34
  162.9 25.8 %fusion = f32[2,10,64,512]{3,2,1,0:T(8,128)S(1)} fusion(f32[10,2,512,512]{3,2,1,0:T(8,128)} %gather_fusion.2, f32[10,2,64,512]{3,2,1,0:T(8,128)} %gather_fusion.1), kind=kOutput, calls=%fused_computation.3 | convolution fusion | flops 4026531840 | bytes 26214400 | tf_op jit(solution)/shard_map/sprv,spmv->sprm/dot_general | solution.py:35
  188.7 3.9 %fusion.5 = f32[32,64,512]{2,0,1:T(8,128)S(1)} fusion(f32[2,10,64,512]{3,2,1,0:T(8,128)S(1)} %fusion, s32[2,10]{1,0:T(2,128)S(1)} %copy.14), kind=kOutput, calls=%fused_computation.8 | convolution fusion | flops 251658880 | bytes 6815824 | tf_op jit(solution)/shard_map/spa,sprw->arw/dot_general | solution.py:38
  192.6 4.4 %copy.16 = f32[32,64,512]{2,1,0:T(8,128)} copy(f32[32,64,512]{2,0,1:T(8,128)S(1)} %fusion.5) | data formatting | bytes 8388608 | tf_op jit(solution)/shard_map/spa,sprw->arw/dot_general | solution.py:38
  197.0 0.0 copy-start.2
  197.0 0.0 reduce-scatter.2.cloned.1.call-update
  197.0 88.4 %reduce-scatter.2.cloned.1.call-done = f32[1,64,512]{2,1,0:T(8,128)} async-done(((f32[32,64,512]{2,1,0:T(8,128)}), f32[1,64,512]{2,1,0:T(8,128)}) %reduce-scatter.2.cloned.1.call-update) | async-done | bytes 131088 | tf_op jit(solution)/shard_map/reduce_scatter | solution.py:39
  285.4 0.0 copy-done.2
  285.4 1.6 sub.11
  (3 shorter events, 0.0 us)
Async XLA Ops:
  6.5 1.7 copy-start
  6.5 46.4 %all-gather.3.cloned.1.call-start = ((), (), s32[]{:S(2)}) async-start(), calls=%async_computation.1 | async-start | bytes 2359296 | tf_op jit(solution)/shard_map/all_gather | solution.py:30
  7.3 143.1 %all-gather.5.cloned.1.call-start = ((), (), s32[]{:S(2)}) async-start(), calls=%async_computation.2 | async-start | bytes 9437184 | tf_op jit(solution)/shard_map/all_gather | solution.py:34
  53.0 4.6 %copy-start.3 = (s32[64,10]{0,1:T(8,128)S(1)}, s32[64,10]{0,1:T(8,128)}, u32[]{:S(2)}) copy-start(s32[64,10]{0,1:T(8,128)} %param.12) | copy-start | bytes 7684
  53.0 4.8 %copy-start.5 = (s32[10]{0:T(128)S(1)}, s32[10]{0:T(128)}, u32[]{:S(2)}) copy-start(s32[10]{0:T(128)} %constant.33) | copy-start | bytes 124
  53.0 4.8 %copy-start.4 = (s32[10]{0:T(128)S(1)}, s32[10]{0:T(128)}, u32[]{:S(2)}) copy-start(s32[10]{0:T(128)} %constant.32) | copy-start | bytes 124
  57.5 1.2 copy-start.1
  57.6 227.9 %reduce-scatter.2.cloned.1.call-start = ((), (), s32[]{:S(2)}) async-start(), calls=%async_computation.3 | async-start | bytes 4325376 | tf_op jit(solution)/shard_map/reduce_scatter | solution.py:39
  197.0 88.4 %copy-start.2 = (f32[1,64,512]{2,1,0:T(8,128)S(1)}, f32[1,64,512]{2,1,0:T(8,128)}, u32[]{:S(2)}) copy-start(f32[1,64,512]{2,1,0:T(8,128)} %param.13) | copy-start | bytes 393220
Sparse Core Ops, SparseCore 0:
  9.1 43.8 all-gather.2
  57.7 92.6 all-gather.4
  197.1 88.2 reduce-scatter.1
where the time goes:
time: 294 us
  waiting for transfers between devices  223 us (76%)
  matrix products  34.2 us (12%)
  local copies, waits for them, and re-layouts  21.1 us (7%)
  between operations  13.2 us (4%)
    all_gather x1, waiting for transfers between devices, shards(): lax.all_gather(scaled, 'narrow', axis=2, tiled=True)[:, right_pick]  89.4 us
    reduce_scatter x1, waiting for transfers between devices, shards(): totals = lax.psum_scatter(portion, 'wide', scatter_dimension=0, tiled=True)  88.4 us
    all_gather x1, waiting for transfers between devices, shards(): full_factors = lax.all_gather(factors, 'narrow', axis=1, tiled=True)  44.1 us
    dot_general x1, matrix products, shards(): jnp.einsum('sprv,spmv->sprm', left_rows, right_rows, precision=highest)  25.8 us
    gather x1, local copies, waits for them, and re-layouts, shards(): lax.all_gather(scaled, 'narrow', axis=2, tiled=True)[:, right_pick]  12.6 us
  transfers between devices with their start and end apart: 3, of which 3 were waited for; matrix products, arithmetic and copies ran while one was open for 1% of the time, Pallas kernels for 0%

commit v1 on v0

--- a/solution.py
+++ b/solution.py
@@ -27,7 +27,25 @@
         - owner_index * blk_count
     )
     own_targets = lax.dynamic_slice_in_dim(target, owner_index * sup_count, sup_count, 0)
-    full_factors = lax.all_gather(factors, "narrow", axis=1, tiled=True)
+    length, index, span = (lax.axis_size("narrow"), lax.axis_index("narrow"), factors.shape[1])
+    forward = [(i, (i + 1) % length) for i in range(length)]
+    left = [(i, (i - 1) % length) for i in range(length)]
+    full_factors = jnp.zeros(
+        (*factors.shape[:1], length * span, *factors.shape[1 + 1 :]), factors.dtype
+    )
+    full_factors = lax.dynamic_update_slice_in_dim(full_factors, factors, index * span, axis=1)
+    from_left = from_right = factors
+    middle = length // 2
+    for step in range(1, middle + 1):
+        from_left = lax.ppermute(from_left, "narrow", forward)
+        full_factors = lax.dynamic_update_slice_in_dim(
+            full_factors, from_left, (index - step) % length * span, axis=1
+        )
+        if step < length - middle:
+            from_right = lax.ppermute(from_right, "narrow", left)
+            full_factors = lax.dynamic_update_slice_in_dim(
+                full_factors, from_right, (index + step) % length * span, axis=1
+            )
     blocks = panels[own_members]
     scaled = jnp.einsum("skrw,swv->skrv", blocks, full_factors, precision=highest)
     left_rows = scaled[:, left_pick]

time: 294 us -> 284 us (0.966)
  waiting for transfers between devices: 223 us -> 196 us
  starting transfers between devices: 0.08 us -> 13.2 us
  local copies, waits for them, and re-layouts: 21.1 us -> 26.1 us
    all_gather x1 -> x0, waiting for transfers between devices: 44.1 us -> none  [shards(): full_factors = lax.all_gather(factors, 'narrow', axis=1, tiled=True)]
    ppermute x0 -> x7, waiting for transfers between devices: none -> 17.3 us  [the longest x4 16.9 us: shards(): from_left = lax.ppermute(from_left, 'narrow', forward)]
    ppermute x0 -> x7, starting transfers between devices: none -> 13 us  [the longest x3 11 us: shards(): from_right = lax.ppermute(from_right, 'narrow', left)]
    dynamic_update_slice x0 -> x8, local copies, waits for them, and re-layouts: none -> 3.97 us  [the longest x4 1.98 us: shards(): lax.dynamic_update_slice_in_dim(full_factors, from_left, (index - step) %...]
  transfers between devices with their start and end apart: 3 -> 9, of which waited for: 3 -> 8; matrix products, arithmetic and copies ran while one was open for 1% -> 3% of each run, Pallas kernels for 0% -> 0%
where the time goes in v1:
time: 284 us
  waiting for transfers between devices  196 us (69%)
  matrix products  32.6 us (11%)
  local copies, waits for them, and re-layouts  26.1 us (9%)
  between operations  13.5 us (5%)
  starting transfers between devices  13.2 us (5%)
    all_gather x1, waiting for transfers between devices, shards(): lax.all_gather(scaled, 'narrow', axis=2, tiled=True)[:, right_pick]  90.4 us
    reduce_scatter x1, waiting for transfers between devices, shards(): totals = lax.psum_scatter(portion, 'wide', scatter_dimension=0, tiled=True)  88.4 us
    dot_general x1, matrix products, shards(): jnp.einsum('sprv,spmv->sprm', left_rows, right_rows, precision=highest)  25.8 us
    ppermute x4, waiting for transfers between devices, shards(): from_left = lax.ppermute(from_left, 'narrow', forward)  16.9 us
    gather x1, local copies, waits for them, and re-layouts, shards(): lax.all_gather(scaled, 'narrow', axis=2, tiled=True)[:, right_pick]  12.6 us
    ppermute x3, starting transfers between devices, shards(): from_right = lax.ppermute(from_right, 'narrow', left)  11 us
  transfers between devices with their start and end apart: 9, of which 8 were waited for; matrix products, arithmetic and copies ran while one was open for 3% of the time, Pallas kernels for 0%

profile of v1, /device:TPU:2, one launch (start us, length us, event | category | flops | bytes accessed | tf_op | source)
XLA Modules:
  0.0 284.0 jit_solution(9113508424395784928)
XLA Ops:
  6.5 0.0 copy-start
  6.5 0.0 all-gather.2.cloned.1.call-start
  6.5 1.9 collective-permute-start
  8.5 3.9 %collective-permute-start.1 = (f32[2,64,512]{2,1,0:T(8,128)}, f32[2,64,512]{2,1,0:T(8,128)S(1)}, u32[]{:S(2)}, u32[]{:S(2)}) collective-permute-start(f32[2,64,512]{2,1,0:T(8,128)} %param.10), channel_id=1, source_target_pairs={{0,7},{1,0},{2,1},{3,2},{4,3},{5,4},{6,5},{7,6},{8,15},{9,8},{10,9... | collective-permute-start | bytes 786440 | tf_op jit(solution)/shard_map/ppermute | solution.py:45
  12.4 6.6 %collective-permute-done = f32[2,64,512]{2,1,0:T(8,128)} collective-permute-done((f32[2,64,512]{2,1,0:T(8,128)}, f32[2,64,512]{2,1,0:T(8,128)}, u32[]{:S(2)}, u32[]{:S(2)}) %collective-permute-start) | collective-permute-done | bytes 262176 | tf_op jit(solution)/shard_map/ppermute | solution.py:40
  19.0 0.0 collective-permute-start.2
  19.0 0.8 compare_select_fusion
  19.8 0.1 copy.15
  19.9 0.1 reshape.3
  20.0 0.2 broadcast_in_dim.15
  20.2 1.0 constant_dynamic-update-slice_fusion.7
  21.2 0.0 collective-permute-done.1
  21.2 3.3 %collective-permute-start.3 = (f32[2,64,512]{2,1,0:T(8,128)S(1)}, f32[2,64,512]{2,1,0:T(8,128)}, u32[]{:S(2)}, u32[]{:S(2)}) collective-permute-start(f32[2,64,512]{2,1,0:T(8,128)S(1)} %collective-permute-done.1), channel_id=1, source_target_pairs={{0,7},{1,0},{2,1},{3,2},{4,3},{5,4},{6,5},{7,6},{8,15},{9,8},{10,9... | collective-permute-start | bytes 786440 | tf_op jit(solution)/shard_map/ppermute | solution.py:45
  24.5 0.0 copy-done
  24.5 1.6 gather_fusion
  26.1 0.0 copy-start.2
  26.1 1.9 collective-permute-done.2
  28.0 0.0 collective-permute-start.4
  28.0 1.0 constant_dynamic-update-slice_fusion.6
  29.0 0.2 collective-permute-done.3
  29.2 3.8 %collective-permute-start.5 = (f32[2,64,512]{2,1,0:T(8,128)}, f32[2,64,512]{2,1,0:T(8,128)S(1)}, u32[]{:S(2)}, u32[]{:S(2)}) collective-permute-start(f32[2,64,512]{2,1,0:T(8,128)} %collective-permute-done.3), channel_id=1, source_target_pairs={{0,7},{1,0},{2,1},{3,2},{4,3},{5,4},{6,5},{7,6},{8,15},{9,8},{10,9... | collective-permute-start | bytes 786440 | tf_op jit(solution)/shard_map/ppermute | solution.py:45
  33.0 1.0 constant_dynamic-update-slice_fusion.4
  34.0 2.1 collective-permute-done.4
  36.0 0.0 collective-permute-start.6
  36.1 1.0 constant_dynamic-update-slice_fusion.3
  37.1 0.2 collective-permute-done.5
  37.3 6.4 %collective-permute-done.6 = f32[2,64,512]{2,1,0:T(8,128)S(1)} collective-permute-done((f32[2,64,512]{2,1,0:T(8,128)S(1)}, f32[2,64,512]{2,1,0:T(8,128)S(1)}, u32[]{:S(2)}, u32[]{:S(2)}) %collective-permute-start.6) | collective-permute-done | bytes 262176 | tf_op jit(solution)/shard_map/ppermute | solution.py:40
  43.7 0.0 copy-done.2
  43.7 0.0 copy-start.4
  43.7 0.0 copy-start.6
  43.7 0.0 copy-start.5
  43.7 2.9 %fusion.8 = f32[2,4,64,512]{3,2,1,0:T(8,128)} fusion(f32[2,4,64,512]{3,2,1,0:T(8,128)S(1)} %bitcast.21, f32[2,512,512]{2,1,0:T(8,128)S(1)} %constant_dynamic-update-slice_fusion), kind=kOutput, calls=%fused_computation.9 | convolution fusion | flops 1610612736 | bytes 4194304 | tf_op jit(solution)/shard_map/skrw,swv->skrv/dot_general | solution.py:50
  46.6 0.0 copy-start.1
  46.6 0.0 all-gather.2.cloned.1.call-update
  46.7 0.2 reduce-scatter.2.cloned.1.call-start
  46.9 0.0 copy-done.4
  46.9 0.1 constant_dynamic-slice_fusion.1
  47.0 0.1 copy.14
  47.1 0.0 copy-done.6
  47.1 0.0 copy-done.5
  47.1 0.8 copy-done.1
  47.9 2.2 gather_fusion.1
  50.0 90.4 %all-gather.2.cloned.1.call-done = f32[2,4,512,512]{3,2,1,0:T(8,128)} async-done(((f32[2,4,64,512]{3,2,1,0:T(8,128)}), f32[2,4,512,512]{3,2,1,0:T(8,128)}) %all-gather.2.cloned.1.call-update) | async-done | bytes 8388624 | tf_op jit(solution)/shard_map/all_gather | solution.py:52
  140.4 12.6 %gather_fusion.2 = f32[10,2,512,512]{3,2,1,0:T(8,128)} fusion(f32[2,4,512,512]{3,2,1,0:T(8,128)} %all-gather.2.cloned.1.call-done, s32[1024]{0:T(1024)S(1)} %pad_clamp_fusion), kind=kCustom, calls=%fused_computation.2 | custom fusion | bytes 41943080 | tf_op jit(solution)/shard_map/gather | solution.py:52
  153.0 25.8 %fusion = f32[2,10,64,512]{3,2,1,0:T(8,128)S(1)} fusion(f32[10,2,512,512]{3,2,1,0:T(8,128)} %gather_fusion.2, f32[10,2,64,512]{3,2,1,0:T(8,128)} %gather_fusion.1), kind=kOutput, calls=%fused_computation.3 | convolution fusion | flops 4026531840 | bytes 26214400 | tf_op jit(solution)/shard_map/sprv,spmv->sprm/dot_general | solution.py:53
  178.8 3.9 %fusion.5 = f32[32,64,512]{2,0,1:T(8,128)S(1)} fusion(f32[2,10,64,512]{3,2,1,0:T(8,128)S(1)} %fusion, s32[2,10]{1,0:T(2,128)S(1)} %copy.14), kind=kOutput, calls=%fused_computation.8 | convolution fusion | flops 251658880 | bytes 6815824 | tf_op jit(solution)/shard_map/spa,sprw->arw/dot_general | solution.py:56
  182.7 4.4 %copy.16 = f32[32,64,512]{2,1,0:T(8,128)} copy(f32[32,64,512]{2,0,1:T(8,128)S(1)} %fusion.5) | data formatting | bytes 8388608 | tf_op jit(solution)/shard_map/spa,sprw->arw/dot_general | solution.py:56
  187.1 0.0 copy-start.3
  187.1 0.0 reduce-scatter.2.cloned.1.call-update
  187.1 88.4 %reduce-scatter.2.cloned.1.call-done = f32[1,64,512]{2,1,0:T(8,128)} async-done(((f32[32,64,512]{2,1,0:T(8,128)}), f32[1,64,512]{2,1,0:T(8,128)}) %reduce-scatter.2.cloned.1.call-update) | async-done | bytes 131088 | tf_op jit(solution)/shard_map/reduce_scatter | solution.py:57
  275.6 0.0 copy-done.3
  275.6 1.6 sub.27
  (7 shorter events, 0.1 us)
Async XLA Ops:
  6.5 18.0 %copy-start = (f32[8,64,512]{2,1,0:T(8,128)S(1)}, f32[8,64,512]{2,1,0:T(8,128)}, u32[]{:S(2)}) copy-start(f32[8,64,512]{2,1,0:T(8,128)} %param.9) | copy-start | bytes 3145732
  6.5 133.9 %all-gather.2.cloned.1.call-start = ((), (), s32[]{:S(2)}) async-start(), calls=%async_computation.1 | async-start | bytes 9437184 | tf_op jit(solution)/shard_map/all_gather | solution.py:52
  6.5 12.5 %collective-permute-start = (f32[2,64,512]{2,1,0:T(8,128)}, f32[2,64,512]{2,1,0:T(8,128)}, u32[]{:S(2)}, u32[]{:S(2)}) collective-permute-start(f32[2,64,512]{2,1,0:T(8,128)} %param.10), channel_id=1, source_target_pairs={{0,1},{1,2},{2,3},{3,4},{4,5},{5,6},{6,7},{7,0},{8,9},{9,10},{10,1... | collective-permute-start | bytes 786440 | tf_op jit(solution)/shard_map/ppermute | solution.py:40
  8.5 12.7 %collective-permute-start.1 = (f32[2,64,512]{2,1,0:T(8,128)}, f32[2,64,512]{2,1,0:T(8,128)S(1)}, u32[]{:S(2)}, u32[]{:S(2)}) collective-permute-start(f32[2,64,512]{2,1,0:T(8,128)} %param.10), channel_id=1, source_target_pairs={{0,7},{1,0},{2,1},{3,2},{4,3},{5,4},{6,5},{7,6},{8,15},{9,8},{10,9... | collective-permute-start | bytes 786440 | tf_op jit(solution)/shard_map/ppermute | solution.py:45
  19.0 9.0 %collective-permute-start.2 = (f32[2,64,512]{2,1,0:T(8,128)}, f32[2,64,512]{2,1,0:T(8,128)}, u32[]{:S(2)}, u32[]{:S(2)}) collective-permute-start(f32[2,64,512]{2,1,0:T(8,128)} %collective-permute-done), channel_id=1, source_target_pairs={{0,1},{1,2},{2,3},{3,4},{4,5},{5,6},{6,7},{7,0},{8,9},{9,10},{10,1... | collective-permute-start | bytes 786440 | tf_op jit(solution)/shard_map/ppermute | solution.py:40
  21.2 8.0 %collective-permute-start.3 = (f32[2,64,512]{2,1,0:T(8,128)S(1)}, f32[2,64,512]{2,1,0:T(8,128)}, u32[]{:S(2)}, u32[]{:S(2)}) collective-permute-start(f32[2,64,512]{2,1,0:T(8,128)S(1)} %collective-permute-done.1), channel_id=1, source_target_pairs={{0,7},{1,0},{2,1},{3,2},{4,3},{5,4},{6,5},{7,6},{8,15},{9,8},{10,9... | collective-permute-start | bytes 786440 | tf_op jit(solution)/shard_map/ppermute | solution.py:45
  26.1 17.5 %copy-start.2 = (f32[8,64,512]{2,1,0:T(8,128)S(1)}, f32[8,64,512]{2,1,0:T(8,128)}, u32[]{:S(2)}) copy-start(f32[8,64,512]{2,1,0:T(8,128)} %gather_fusion) | copy-start | bytes 3145732
  28.0 8.0 %collective-permute-start.4 = (f32[2,64,512]{2,1,0:T(8,128)}, f32[2,64,512]{2,1,0:T(8,128)S(1)}, u32[]{:S(2)}, u32[]{:S(2)}) collective-permute-start(f32[2,64,512]{2,1,0:T(8,128)} %collective-permute-done.2), channel_id=1, source_target_pairs={{0,1},{1,2},{2,3},{3,4},{4,5},{5,6},{6,7},{7,0},{8,9},{9,10},{10,1... | collective-permute-start | bytes 786440 | tf_op jit(solution)/shard_map/ppermute | solution.py:40
  29.2 8.0 %collective-permute-start.5 = (f32[2,64,512]{2,1,0:T(8,128)}, f32[2,64,512]{2,1,0:T(8,128)S(1)}, u32[]{:S(2)}, u32[]{:S(2)}) collective-permute-start(f32[2,64,512]{2,1,0:T(8,128)} %collective-permute-done.3), channel_id=1, source_target_pairs={{0,7},{1,0},{2,1},{3,2},{4,3},{5,4},{6,5},{7,6},{8,15},{9,8},{10,9... | collective-permute-start | bytes 786440 | tf_op jit(solution)/shard_map/ppermute | solution.py:45
  36.0 7.6 %collective-permute-start.6 = (f32[2,64,512]{2,1,0:T(8,128)S(1)}, f32[2,64,512]{2,1,0:T(8,128)S(1)}, u32[]{:S(2)}, u32[]{:S(2)}) collective-permute-start(f32[2,64,512]{2,1,0:T(8,128)S(1)} %collective-permute-done.4), channel_id=1, source_target_pairs={{0,1},{1,2},{2,3},{3,4},{4,5},{5,6},{6,7},{7,0},{8,9},{9,10},{10,1... | collective-permute-start | bytes 786440 | tf_op jit(solution)/shard_map/ppermute | solution.py:40
  43.7 3.2 %copy-start.4 = (s32[64,10]{0,1:T(8,128)S(1)}, s32[64,10]{0,1:T(8,128)}, u32[]{:S(2)}) copy-start(s32[64,10]{0,1:T(8,128)} %param.12) | copy-start | bytes 7684
  43.7 3.4 %copy-start.6 = (s32[10]{0:T(128)S(1)}, s32[10]{0:T(128)}, u32[]{:S(2)}) copy-start(s32[10]{0:T(128)} %constant.87) | copy-start | bytes 124
  43.7 3.4 %copy-start.5 = (s32[10]{0:T(128)S(1)}, s32[10]{0:T(128)}, u32[]{:S(2)}) copy-start(s32[10]{0:T(128)} %constant.86) | copy-start | bytes 124
  46.6 1.2 copy-start.1
  46.7 228.9 %reduce-scatter.2.cloned.1.call-start = ((), (), s32[]{:S(2)}) async-start(), calls=%async_computation.2 | async-start | bytes 4325376 | tf_op jit(solution)/shard_map/reduce_scatter | solution.py:57
  187.1 88.4 %copy-start.3 = (f32[1,64,512]{2,1,0:T(8,128)S(1)}, f32[1,64,512]{2,1,0:T(8,128)}, u32[]{:S(2)}) copy-start(f32[1,64,512]{2,1,0:T(8,128)} %param.13) | copy-start | bytes 393220
Sparse Core Ops, SparseCore 0:
  46.8 93.5 all-gather.1
  187.3 88.2 reduce-scatter.1
